TPU v7x, 32 devices: a whole 2x2x4 slice. The times are simulated.
32 devices in a mesh: rep: 2 (over y), shard: 16 (over z, x, core).
Axes of the slice: x: 2, y: 2, z: 4, core: 2. Of those that a mesh axis runs over, the one named last changes fastest.
Arguments:
- latents: bfloat16 [32, 128, 1152], P(('rep', 'shard')), may hold values from -5 to 5
- cond: float32 [32, 1152], P(('rep', 'shard')), may hold values from -6 to 6
- timesteps: int32 [32], P(('rep', 'shard')), may hold values from 0 to 999
- cotangent: bfloat16 [32, 128, 1152], P(('rep', 'shard')), may hold values from -6 to 6
- w_qkv: float32 [1152, 3456], P('shard'), may hold values from -0.11785113 to 0.11785113
- w_proj: float32 [1152, 1152], P('shard'), may hold values from -0.75 to 0.75
- w_fc1: float32 [1152, 4608], P('shard'), may hold values from -0.1875 to 0.1875
- w_fc2: float32 [4608, 1152], P('shard'), may hold values from -0.1875 to 0.1875
- w_ada: float32 [1152, 6912], P(None, 'shard'), may hold values from -0.015625 to 0.015625
- biases: float32 [16128], replicated, may hold values from -3 to 3
- m_qkv: float32 [1152, 3456], P('shard', 'rep'), may hold values from -0.00012272017 to 0.00012272017
- m_proj: float32 [1152, 1152], P('shard', 'rep'), may hold values from -0.00012272017 to 0.00012272017
- m_fc1: float32 [1152, 4608], P('shard', 'rep'), may hold values from -0.00012272017 to 0.00012272017
- m_fc2: float32 [4608, 1152], P('shard', 'rep'), may hold values from -0.00012272017 to 0.00012272017
- m_ada: float32 [1152, 6912], P('rep', 'shard'), may hold values from -0.00012272017 to 0.00012272017
- m_bias: float32 [16128], replicated, may hold values from -0.00012272017 to 0.00012272017
- v_qkv: float32 [1152, 3456], P('shard', 'rep'), may hold values from 4.1834e-11 to 1.67336e-10
- v_proj: float32 [1152, 1152], P('shard', 'rep'), may hold values from 4.1834e-11 to 1.67336e-10
- v_fc1: float32 [1152, 4608], P('shard', 'rep'), may hold values from 4.1834e-11 to 1.67336e-10
- v_fc2: float32 [4608, 1152], P('shard', 'rep'), may hold values from 4.1834e-11 to 1.67336e-10
- v_ada: float32 [1152, 6912], P('rep', 'shard'), may hold values from 4.1834e-11 to 1.67336e-10
- v_bias: float32 [16128], replicated, may hold values from 4.1834e-11 to 1.67336e-10
Outputs:
- block_out: float32 [32, 128, 1152], P(('rep', 'shard'))
- latents_grad: float32 [32, 128, 1152], P(('rep', 'shard'))
- cond_grad: float32 [32, 1152], P(('rep', 'shard'))
- new_qkv: float32 [1152, 3456], P('shard')
- new_proj: float32 [1152, 1152], P('shard')
- new_fc1: float32 [1152, 4608], P('shard')
- new_fc2: float32 [4608, 1152], P('shard')
- new_ada: float32 [1152, 6912], P(None, 'shard')
- bias_update: float32 [16128], replicated
- new_m_qkv: float32 [1152, 3456], P('shard', 'rep')
- new_m_proj: float32 [1152, 1152], P('shard', 'rep')
- new_m_fc1: float32 [1152, 4608], P('shard', 'rep')
- new_m_fc2: float32 [4608, 1152], P('shard', 'rep')
- new_m_ada: float32 [1152, 6912], P('rep', 'shard')
- new_m_bias: float32 [16128], replicated
- new_v_qkv: float32 [1152, 3456], P('shard', 'rep')
- new_v_proj: float32 [1152, 1152], P('shard', 'rep')
- new_v_fc1: float32 [1152, 4608], P('shard', 'rep')
- new_v_fc2: float32 [4608, 1152], P('shard', 'rep')
- new_v_ada: float32 [1152, 6912], P('rep', 'shard')
- new_v_bias: float32 [16128], replicated
All inputs are finite; a program needn't handle non-finite values.
Results may differ from a plain program's by a relative error of at most 0.014.
Values may be sent and summed in bfloat16 or wider, within the bound.
No kernel may reach another device: no remote copies, remote signals or barrier semaphores. Data moves between devices by JAX's collectives and lax.ppermute only.
A program may use at most 256 MiB of HBM per device.

v0:
```python
import math
import jax
import jax.numpy as jnp
from jax import lax
from jax.sharding import PartitionSpec as P

HD = 72
H = 16
FF = 4608
ln_eps = 1e-06
beta_one = 0.9
beta_two = 0.999
adam_eps = 1e-08
learn_rate = 0.03
decay_rate = 0.01
step_count = 2
gelu_coef = 0.044715


def product(form, left, right):
    return jnp.einsum(form, left, right, preferred_element_type=jnp.float32)


def normalize(rows):
    center = rows - jnp.mean(rows, axis=-1, keepdims=True)
    rstd = lax.rsqrt(jnp.mean(center * center, axis=-1, keepdims=True) + ln_eps)
    return (center * rstd, rstd)


def norm_back(grad, normed, rstd):
    return rstd * (
        grad
        - jnp.mean(grad, axis=-1, keepdims=True)
        - normed * jnp.mean(grad * normed, axis=-1, keepdims=True)
    )


def gelu_parts(pre):
    root = math.sqrt(2.0 / math.pi)
    inner = root * (pre + gelu_coef * pre * pre * pre)
    tangent = jnp.tanh(inner)
    value = 0.5 * pre * (1.0 + tangent)
    slope = 0.5 * (1.0 + tangent) + 0.5 * pre * (1.0 - tangent * tangent) * root * (
        1.0 + 3.0 * gelu_coef * pre * pre
    )
    return (value, slope)


def time_embed(steps, width):
    half = width // 2
    freqs = jnp.exp(-math.log(10000.0) * jnp.arange(half, dtype=jnp.float32) / half)
    angles = steps.astype(jnp.float32)[:, None] * freqs[None, :]
    return jnp.concatenate([jnp.cos(angles), jnp.sin(angles)], axis=1)


def block_pass(inputs, cotan, mod, wq_b, wp_b, w1_b, w2_b, biases):
    batch, length, width = inputs.shape
    inner = H * HD
    b_q = biases[0:inner]
    b_v = biases[inner : 2 * inner]
    b_proj = biases[2 * inner : 2 * inner + width]
    b_fc1 = biases[2 * inner + width : 2 * inner + width + FF]
    b_fc2 = biases[2 * inner + width + FF : 2 * inner + 2 * width + FF]
    parts = [mod[:, i * width : (i + 1) * width][:, None, :] for i in range(6)]
    shift1, scale1, gate1, shift2, scale2, gate2 = parts
    rows = inputs.astype(jnp.float32)
    n_one, r_one = normalize(rows)
    a_one = (n_one * (1.0 + scale1) + shift1).astype(jnp.bfloat16)
    qkv = product("bld,de->ble", a_one, wq_b)
    queries = (qkv[..., :inner] + b_q).astype(jnp.bfloat16).reshape(batch, length, H, HD)
    key_rows = qkv[..., inner : 2 * inner].astype(jnp.bfloat16).reshape(batch, length, H, HD)
    value_rows = (qkv[..., 2 * inner :] + b_v).astype(jnp.bfloat16).reshape(batch, length, H, HD)
    factor = HD ** (-0.5)
    scores = product("bqhd,bkhd->bhqk", queries, key_rows) * factor
    top = jnp.max(scores, axis=-1, keepdims=True)
    expo = jnp.exp(scores - top)
    probs = expo / jnp.sum(expo, axis=-1, keepdims=True)
    probs_b = probs.astype(jnp.bfloat16)
    heads_out = product("bhqk,bkhd->bqhd", probs_b, value_rows).astype(jnp.bfloat16)
    heads_flat = heads_out.reshape(batch, length, inner)
    attn = product("ble,ed->bld", heads_flat, wp_b) + b_proj
    x_one = rows + gate1 * attn
    n_two, r_two = normalize(x_one)
    a_two = (n_two * (1.0 + scale2) + shift2).astype(jnp.bfloat16)
    pre = product("bld,df->blf", a_two, w1_b) + b_fc1
    act_val, act_slope = gelu_parts(pre)
    act = act_val.astype(jnp.bfloat16)
    mlp = product("blf,fd->bld", act, w2_b) + b_fc2
    out = x_one + gate2 * mlp
    grad_out = cotan.astype(jnp.float32)
    d_gate2 = jnp.sum(grad_out * mlp, axis=1)
    d_mlp = grad_out * gate2
    d_mlp_b = d_mlp.astype(jnp.bfloat16)
    g_fc2 = product("blf,bld->fd", act, d_mlp_b)
    g_b_fc2 = jnp.sum(d_mlp, axis=(0, 1))
    d_pre = product("bld,fd->blf", d_mlp_b, w2_b) * act_slope
    d_pre_b = d_pre.astype(jnp.bfloat16)
    g_fc1 = product("bld,blf->df", a_two, d_pre_b)
    g_b_fc1 = jnp.sum(d_pre, axis=(0, 1))
    d_a2 = product("blf,df->bld", d_pre_b, w1_b)
    d_shift2 = jnp.sum(d_a2, axis=1)
    d_scale2 = jnp.sum(d_a2 * n_two, axis=1)
    dx_one = grad_out + norm_back(d_a2 * (1.0 + scale2), n_two, r_two)
    d_gate1 = jnp.sum(dx_one * attn, axis=1)
    d_attn = dx_one * gate1
    d_attn_b = d_attn.astype(jnp.bfloat16)
    g_proj = product("ble,bld->ed", heads_flat, d_attn_b)
    g_b_proj = jnp.sum(d_attn, axis=(0, 1))
    d_heads = (
        product("bld,ed->ble", d_attn_b, wp_b).astype(jnp.bfloat16).reshape(batch, length, H, HD)
    )
    delta = jnp.sum(d_heads.astype(jnp.float32) * heads_out.astype(jnp.float32), axis=-1)
    delta = jnp.transpose(delta, (0, 2, 1))[..., None]
    d_probs = product("bqhd,bkhd->bhqk", d_heads, value_rows)
    d_scores = (probs * (d_probs - delta) * factor).astype(jnp.bfloat16)
    d_q = product("bhqk,bkhd->bqhd", d_scores, key_rows)
    d_k = product("bhqk,bqhd->bkhd", d_scores, queries)
    d_v = product("bhqk,bqhd->bkhd", probs_b, d_heads)
    g_b_q = jnp.sum(d_q, axis=(0, 1)).reshape(inner)
    g_b_v = jnp.sum(d_v, axis=(0, 1)).reshape(inner)
    d_qkv = jnp.concatenate(
        [
            d_q.reshape(batch, length, inner),
            d_k.reshape(batch, length, inner),
            d_v.reshape(batch, length, inner),
        ],
        axis=-1,
    ).astype(jnp.bfloat16)
    g_qkv = product("bld,ble->de", a_one, d_qkv)
    d_a1 = product("ble,de->bld", d_qkv, wq_b)
    d_shift1 = jnp.sum(d_a1, axis=1)
    d_scale1 = jnp.sum(d_a1 * n_one, axis=1)
    d_input = dx_one + norm_back(d_a1 * (1.0 + scale1), n_one, r_one)
    d_mod = jnp.concatenate([d_shift1, d_scale1, d_gate1, d_shift2, d_scale2, d_gate2], axis=1)
    bias_grad = jnp.concatenate([g_b_q, g_b_v, g_b_proj, g_b_fc1, g_b_fc2])
    return (out, d_input, d_mod, (g_qkv, g_proj, g_fc1, g_fc2), bias_grad)


def adam_change(weight, grad, first, second, clip):
    scaled = grad * clip
    first_new = beta_one * first + (1.0 - beta_one) * scaled
    second_new = beta_two * second + (1.0 - beta_two) * scaled * scaled
    first_hat = first_new / (1.0 - beta_one**step_count)
    second_hat = second_new / (1.0 - beta_two**step_count)
    change = -learn_rate * (first_hat / (jnp.sqrt(second_hat) + adam_eps) + decay_rate * weight)
    return (change, first_new, second_new)


def adam_step(weight, grad, first, second, clip):
    change, first_new, second_new = adam_change(weight, grad, first, second, clip)
    return (weight + change, first_new, second_new)


def shards(
    latents,
    cond,
    timesteps,
    cotangent,
    w_qkv,
    w_proj,
    w_fc1,
    w_fc2,
    w_ada,
    biases,
    m_qkv,
    m_proj,
    m_fc1,
    m_fc2,
    m_ada,
    m_bias,
    v_qkv,
    v_proj,
    v_fc1,
    v_fc2,
    v_ada,
    v_bias,
):
    width = cond.shape[1]
    b_ada = biases[biases.shape[0] - 6 * width :]
    cvec = cond + time_embed(timesteps, width)
    silu_c = jax.nn.silu(cvec).astype(jnp.bfloat16)
    ada_local = w_ada.astype(jnp.bfloat16)
    silu_group = lax.all_gather(silu_c, "shard", axis=0, tiled=True)
    mod_cols = jnp.dot(silu_group, ada_local, preferred_element_type=jnp.float32)
    mod = lax.all_to_all(mod_cols, "shard", split_axis=0, concat_axis=1, tiled=True) + b_ada
    wq_b, wp_b = (
        lax.all_gather(w_qkv.astype(jnp.bfloat16), "shard", axis=0, tiled=True),
        lax.all_gather(w_proj.astype(jnp.bfloat16), "shard", axis=0, tiled=True),
    )
    w1_b, w2_b = (
        lax.all_gather(w_fc1.astype(jnp.bfloat16), "shard", axis=0, tiled=True),
        lax.all_gather(w_fc2.astype(jnp.bfloat16), "shard", axis=0, tiled=True),
    )
    block_out, latents_grad, d_mod, grads, bias_head = block_pass(
        latents, cotangent, mod, wq_b, wp_b, w1_b, w2_b, biases
    )
    d_mod_b = d_mod.astype(jnp.bfloat16)
    d_mod_cols = lax.all_to_all(d_mod_b, "shard", split_axis=1, concat_axis=0, tiled=True)
    g_ada = jnp.dot(silu_group.T, d_mod_cols, preferred_element_type=jnp.float32)
    silu_terms = jnp.dot(d_mod_cols, ada_local.T, preferred_element_type=jnp.float32)
    silu_grad = lax.psum_scatter(silu_terms, "shard", scatter_dimension=0, tiled=True)
    sig = jax.nn.sigmoid(cvec)
    cond_grad = silu_grad * sig * (1.0 + cvec * (1.0 - sig))
    g_qkv, g_proj = (
        lax.psum_scatter(
            grads[0].astype(jnp.bfloat16), "shard", scatter_dimension=0, tiled=True
        ).astype(jnp.float32),
        lax.psum_scatter(
            grads[1].astype(jnp.bfloat16), "shard", scatter_dimension=0, tiled=True
        ).astype(jnp.float32),
    )
    g_fc1, g_fc2 = (
        lax.psum_scatter(
            grads[2].astype(jnp.bfloat16), "shard", scatter_dimension=0, tiled=True
        ).astype(jnp.float32),
        lax.psum_scatter(
            grads[3].astype(jnp.bfloat16), "shard", scatter_dimension=0, tiled=True
        ).astype(jnp.float32),
    )
    pieces = (
        lax.psum_scatter(g_qkv, "rep", scatter_dimension=1, tiled=True),
        lax.psum_scatter(g_proj, "rep", scatter_dimension=1, tiled=True),
        lax.psum_scatter(g_fc1, "rep", scatter_dimension=1, tiled=True),
        lax.psum_scatter(g_fc2, "rep", scatter_dimension=1, tiled=True),
        lax.psum_scatter(g_ada, "rep", scatter_dimension=0, tiled=True),
    )
    bias_partial = jnp.concatenate([bias_head, jnp.sum(d_mod, axis=0)])
    weight_squares = sum((jnp.sum(p * p) for p in pieces))
    g_bias, total_squares = lax.psum((bias_partial, weight_squares), ("rep", "shard"))
    gnorm = jnp.sqrt(total_squares + jnp.sum(g_bias * g_bias))
    clip = 1.0 / jnp.maximum(gnorm, 1.0)
    rank = lax.axis_index("rep")
    replicas = lax.axis_size("rep")
    weights = (w_qkv, w_proj, w_fc1, w_fc2, w_ada)
    dims = (1, 1, 1, 1, 0)
    firsts = (m_qkv, m_proj, m_fc1, m_fc2, m_ada)
    seconds = (v_qkv, v_proj, v_fc1, v_fc2, v_ada)
    new_pieces = []
    new_m = []
    new_v = []
    for weight, dim, grad, first, second in zip(weights, dims, pieces, firsts, seconds):
        count = weight.shape[dim] // replicas
        own = lax.dynamic_slice_in_dim(weight, rank * count, count, dim)
        updated, first_new, second_new = adam_step(own, grad, first, second, clip)
        new_pieces.append(updated)
        new_m.append(first_new)
        new_v.append(second_new)
    new_qkv, new_proj, new_fc1, new_fc2, new_ada = (
        lax.all_gather(new_pieces[0], "rep", axis=1, tiled=True),
        lax.all_gather(new_pieces[1], "rep", axis=1, tiled=True),
        lax.all_gather(new_pieces[2], "rep", axis=1, tiled=True),
        lax.all_gather(new_pieces[3], "rep", axis=1, tiled=True),
        lax.all_gather(new_pieces[4], "rep", axis=0, tiled=True),
    )
    bias_update, new_m_bias, new_v_bias = adam_change(biases, g_bias, m_bias, v_bias, clip)
    return (
        block_out,
        latents_grad,
        cond_grad,
        new_qkv,
        new_proj,
        new_fc1,
        new_fc2,
        new_ada,
        bias_update,
        new_m[0],
        new_m[1],
        new_m[2],
        new_m[3],
        new_m[4],
        new_m_bias,
        new_v[0],
        new_v[1],
        new_v[2],
        new_v[3],
        new_v[4],
        new_v_bias,
    )


def solution(mesh):
    in_specs = (
        P(("rep", "shard"), None, None),
        P(("rep", "shard"), None),
        P(("rep", "shard")),
        P(("rep", "shard"), None, None),
        P("shard", None),
        P("shard", None),
        P("shard", None),
        P("shard", None),
        P(None, "shard"),
        P(),
        P("shard", "rep"),
        P("shard", "rep"),
        P("shard", "rep"),
        P("shard", "rep"),
        P("rep", "shard"),
        P(),
        P("shard", "rep"),
        P("shard", "rep"),
        P("shard", "rep"),
        P("shard", "rep"),
        P("rep", "shard"),
        P(),
    )
    out_specs = (
        P(("rep", "shard"), None, None),
        P(("rep", "shard"), None, None),
        P(("rep", "shard"), None),
        P("shard", None),
        P("shard", None),
        P("shard", None),
        P("shard", None),
        P(None, "shard"),
        P(),
        P("shard", "rep"),
        P("shard", "rep"),
        P("shard", "rep"),
        P("shard", "rep"),
        P("rep", "shard"),
        P(),
        P("shard", "rep"),
        P("shard", "rep"),
        P("shard", "rep"),
        P("shard", "rep"),
        P("rep", "shard"),
        P(),
    )
    return jax.shard_map(shards, mesh=mesh, in_specs=in_specs, out_specs=out_specs, check_vma=False)
```

profile of v0, /device:TPU:0, one launch (start us, length us, event | category | flops | bytes accessed | tf_op | source)
XLA Modules:
  0.0 1095.6 jit_solution(5412278712987913531)
XLA Ops:
  17.3 24.2 %all-gather = bf16[16,1,1152]{2,1,0:T(2,128)(2,1)S(1)} all-gather(bf16[1,1,1152]{2,1,0:T(2,128)(2,1)S(1)} %get-tuple-element.62), channel_id=1, replica_groups=mesh['rep'=2,'shard'=16] {'shard'}, dimensions={0}, use_global_device_ids=true | all-gather | bytes 39168 | tf_op jit(solution)/shard_map/all_gather | solution.py:183
  54.2 31.5 %all-gather.13.cloned.1.call-done = bf16[1152,3456]{1,0:T(8,128)(2,1)} async-done(((bf16[72,3456]{1,0:T(8,128)(2,1)}), bf16[1152,3456]{1,0:T(8,128)(2,1)}) %all-gather.13.cloned.1.call-update) | async-done | bytes 7962640 | tf_op jit(solution)/shard_map/all_gather | solution.py:187
  92.1 38.2 %all-gather.15.cloned.1.call-done = bf16[1152,1152]{1,0:T(8,128)(2,1)} async-done(((bf16[72,1152]{1,0:T(8,128)(2,1)}), bf16[1152,1152]{1,0:T(8,128)(2,1)}) %all-gather.15.cloned.1.call-update) | async-done | bytes 2654224 | tf_op jit(solution)/shard_map/all_gather | solution.py:188
  134.3 86.1 %all-gather.17.cloned.1.call-done = bf16[1152,4608]{1,0:T(8,128)(2,1)} async-done(((bf16[72,4608]{1,0:T(8,128)(2,1)}), bf16[1152,4608]{1,0:T(8,128)(2,1)}) %all-gather.17.cloned.1.call-update) | async-done | bytes 10616848 | tf_op jit(solution)/shard_map/all_gather | solution.py:191
  226.2 83.5 %all-gather.19.cloned.1.call-done = bf16[4608,1152]{1,0:T(8,128)(2,1)} async-done(((bf16[288,1152]{1,0:T(8,128)(2,1)}), bf16[4608,1152]{1,0:T(8,128)(2,1)}) %all-gather.19.cloned.1.call-update) | async-done | bytes 10616848 | tf_op jit(solution)/shard_map/all_gather | solution.py:192
  309.7 8.6 fusion.93
  323.2 8.2 fusion.19
  354.4 6.7 convolution_convert_fusion
  369.2 6.5 fusion.28
  378.8 9.4 all_to_all.29
  397.9 99.9 %reduce-scatter.36.cloned.1.call-done = bf16[72,3456]{1,0:T(8,128)(2,1)} async-done(((bf16[1152,3456]{1,0:T(8,128)(2,1)}), bf16[72,3456]{1,0:T(8,128)(2,1)}) %reduce-scatter.36.cloned.1.call-update) | async-done | bytes 497680
  500.4 121.8 %reduce-scatter.26.cloned.1.call-done = bf16[288,1152]{1,0:T(8,128)(2,1)} async-done(((bf16[4608,1152]{1,0:T(8,128)(2,1)}), bf16[288,1152]{1,0:T(8,128)(2,1)}) %reduce-scatter.26.cloned.1.call-update) | async-done | bytes 663568 | tf_op jit(solution)/shard_map/reduce_scatter | solution.py:216
  624.9 121.7 %reduce-scatter.22.cloned.1.call-done = bf16[72,4608]{1,0:T(8,128)(2,1)} async-done(((bf16[1152,4608]{1,0:T(8,128)(2,1)}), bf16[72,4608]{1,0:T(8,128)(2,1)}) %reduce-scatter.22.cloned.1.call-update) | async-done | bytes 663568 | tf_op jit(solution)/shard_map/reduce_scatter | solution.py:213
  750.2 33.1 %reduce-scatter.34.cloned.1.call-done = f32[576,432]{1,0:T(8,128)} async-done(((f32[1152,432]{1,0:T(8,128)}), f32[576,432]{1,0:T(8,128)}) %reduce-scatter.34.cloned.1.call-update) | async-done | bytes 995344
  785.8 15.5 %reduce-scatter.30.cloned.1.call-done = f32[576,72]{1,0:T(8,128)} async-done(((f32[1152,72]{1,0:T(8,128)}), f32[576,72]{1,0:T(8,128)}) %reduce-scatter.30.cloned.1.call-update) | async-done | bytes 165904
  804.7 27.8 %reduce-scatter.28.cloned.1.call-done = f32[1728,72]{1,0:T(8,128)} async-done(((f32[3456,72]{1,0:T(8,128)}), f32[1728,72]{1,0:T(8,128)}) %reduce-scatter.28.cloned.1.call-update) | async-done | bytes 497680
  837.8 25.2 %reduce-scatter.32.cloned.1.call-done = f32[576,288]{1,0:T(8,128)} async-done(((f32[1152,288]{1,0:T(8,128)}), f32[576,288]{1,0:T(8,128)}) %reduce-scatter.32.cloned.1.call-update) | async-done | bytes 663568
  867.2 22.1 %reduce-scatter.24.cloned.1.call-done = f32[72,2304]{1,0:T(8,128)} async-done(((f32[72,4608]{1,0:T(8,128)}), f32[72,2304]{1,0:T(8,128)}) %reduce-scatter.24.cloned.1.call-update) | async-done | bytes 663568 | tf_op jit(solution)/shard_map/reduce_scatter | solution.py:223
  893.2 40.0 %all-reduce.3 = (f32[]{:T(128)}, f32[16128]{0:T(1024)S(1)}) all-reduce(f32[]{:T(128)S(6)} %add.349, f32[16128]{0:T(1024)S(1)} %constant_dynamic-update-slice_fusion.10), channel_id=1, replica_groups=mesh['rep'=2,'shard'=16] {'rep','shard'}, use_global_device_ids=true, to_apply=%region_32.33 | all-reduce | flops 16129 | bytes 129032 | tf_op jit(solution)/shard_map/psum | solution.py:229
  949.5 30.8 %all-reduce.6.cloned.1.call-done = f32[16,1152]{1,0:T(8,128)} async-done(((f32[16,1152]{1,0:T(8,128)}), f32[16,1152]{1,0:T(8,128)}) %all-reduce.6.cloned.1.call-update) | async-done | bytes 73744
  985.2 21.1 %all-gather.1 = f32[2,1728,72]{1,2,0:T(8,128)S(1)} all-gather(f32[1,1728,72]{1,2,0:T(8,128)S(1)} %get-tuple-element.56), channel_id=1, replica_groups=mesh['rep'=2,'shard'=16] {'rep'}, dimensions={0}, use_global_device_ids=true | all-gather | bytes 1492992 | tf_op jit(solution)/shard_map/all_gather | solution.py:249
  1009.5 9.2 all-gather.2
  1025.1 19.7 %all-gather.21.cloned.1.call-done = f32[72,4608]{1,0:T(8,128)} async-done(((f32[72,2304]{1,0:T(8,128)}), f32[72,4608]{1,0:T(8,128)}) %all-gather.21.cloned.1.call-update) | async-done | bytes 1327120 | tf_op jit(solution)/shard_map/all_gather | solution.py:251
  1044.9 36.4 %all-gather.25.cloned.1.call-done = f32[2,576,432]{1,2,0:T(8,128)} async-done(((f32[1,576,432]{1,2,0:T(8,128)}), f32[2,576,432]{1,2,0:T(8,128)}) %all-gather.25.cloned.1.call-update) | async-done | bytes 1990672 | tf_op jit(solution)/shard_map/all_gather | solution.py:253
  (280 shorter events, 148.4 us)
Async XLA Ops:
  7.2 78.5 %all-gather.13.cloned.1.call-start = ((), (), s32[]{:S(2)}) async-start(), calls=%async_computation.11 | async-start | bytes 8460288 | tf_op jit(solution)/shard_map/all_gather | solution.py:187
  9.3 121.0 %all-gather.15.cloned.1.call-start = ((), (), s32[]{:S(2)}) async-start(), calls=%async_computation.12 | async-start | bytes 2820096 | tf_op jit(solution)/shard_map/all_gather | solution.py:188
  11.1 209.3 %all-gather.17.cloned.1.call-start = ((), (), s32[]{:S(2)}) async-start(), calls=%async_computation.13 | async-start | bytes 11280384 | tf_op jit(solution)/shard_map/all_gather | solution.py:191
  13.5 296.2 %all-gather.19.cloned.1.call-start = ((), (), s32[]{:S(2)}) async-start(), calls=%async_computation.14 | async-start | bytes 11280384 | tf_op jit(solution)/shard_map/all_gather | solution.py:192
  42.8 10.6 all-to-all-start
  46.3 349.6 %reduce-scatter.38.cloned.1.call-start = ((), (), s32[]{:S(2)}) async-start(), calls=%async_computation.27 | async-start | bytes 2820096
  334.5 163.3 %reduce-scatter.36.cloned.1.call-start = ((), (), s32[]{:S(2)}) async-start(), calls=%async_computation.26 | async-start | bytes 8460288
  354.4 267.8 %reduce-scatter.26.cloned.1.call-start = ((), (), s32[]{:S(2)}) async-start(), calls=%async_computation.17 | async-start | bytes 11280384 | tf_op jit(solution)/shard_map/reduce_scatter | solution.py:216
  361.1 385.5 %reduce-scatter.22.cloned.1.call-start = ((), (), s32[]{:S(2)}) async-start(), calls=%async_computation.15 | async-start | bytes 11280384 | tf_op jit(solution)/shard_map/reduce_scatter | solution.py:213
  368.2 415.1 %reduce-scatter.34.cloned.1.call-start = ((), (), s32[]{:S(2)}) async-start(), calls=%async_computation.24 | async-start | bytes 3538944
  390.3 411.1 %reduce-scatter.30.cloned.1.call-start = ((), (), s32[]{:S(2)}) async-start(), calls=%async_computation.22 | async-start | bytes 884736
  397.8 434.7 %reduce-scatter.28.cloned.1.call-start = ((), (), s32[]{:S(2)}) async-start(), calls=%async_computation.21 | async-start | bytes 2654208
  500.4 362.6 %reduce-scatter.32.cloned.1.call-start = ((), (), s32[]{:S(2)}) async-start(), calls=%async_computation.23 | async-start | bytes 2654208
  624.8 124.2 %copy-start.37 = (f32[16,72]{1,0:T(8,128)S(1)}, f32[16,72]{1,0:T(8,128)}, u32[]{:S(2)}) copy-start(f32[16,72]{1,0:T(8,128)} %get-tuple-element.73) | copy-start | bytes 13828
  624.8 124.3 %copy-start.56 = (f32[16,72]{1,0:T(8,128)S(1)}, f32[16,72]{1,0:T(8,128)}, u32[]{:S(2)}) copy-start(f32[16,72]{1,0:T(8,128)} %get-tuple-element.71) | copy-start | bytes 13828
  624.8 124.4 %copy-start.55 = (f32[1152]{0:T(1024)S(1)}, f32[1152]{0:T(1024)}, u32[]{:S(2)}) copy-start(f32[1152]{0:T(1024)} %get-tuple-element.69) | copy-start | bytes 13828
  624.8 124.5 %copy-start.40 = (f32[4608]{0:T(1024)S(1)}, f32[4608]{0:T(1024)}, u32[]{:S(2)}) copy-start(f32[4608]{0:T(1024)} %get-tuple-element.86) | copy-start | bytes 55300
  624.8 124.5 %copy-start.54 = (f32[1152]{0:T(1024)S(1)}, f32[1152]{0:T(1024)}, u32[]{:S(2)}) copy-start(f32[1152]{0:T(1024)} %get-tuple-element.31) | copy-start | bytes 13828
  624.8 124.5 %copy-start.3 = (f32[1152,432]{0,1:T(8,128)S(1)}, f32[1152,432]{0,1:T(8,128)}, u32[]{:S(2)}) copy-start(f32[1152,432]{0,1:T(8,128)} %param.30) | copy-start | bytes 5971972
  624.9 264.5 %reduce-scatter.24.cloned.1.call-start = ((), (), s32[]{:S(2)}) async-start(), calls=%async_computation.16 | async-start | bytes 1990656 | tf_op jit(solution)/shard_map/reduce_scatter | solution.py:223
  748.9 231.4 %all-reduce.6.cloned.1.call-start = ((), (), s32[]{:S(2)}) async-start(), calls=%async_computation.25 | async-start | bytes 147456
  893.2 127.4 %all-gather.23.cloned.1.call-start = ((), (), s32[]{:S(2)}) async-start(), calls=%async_computation.19 | async-start | bytes 2211840 | tf_op jit(solution)/shard_map/all_gather | solution.py:252
  939.0 105.8 %all-gather.21.cloned.1.call-start = ((), (), s32[]{:S(2)}) async-start(), calls=%async_computation.18 | async-start | bytes 1990656 | tf_op jit(solution)/shard_map/all_gather | solution.py:251
  943.0 138.2 %all-gather.25.cloned.1.call-start = ((), (), s32[]{:S(2)}) async-start(), calls=%async_computation.20 | async-start | bytes 3317760 | tf_op jit(solution)/shard_map/all_gather | solution.py:253
  (62 other events, 751.5 us)
Sparse Core Ops, SparseCore 0:
  10.7 74.9 all-gather.12
  88.5 41.8 all-gather.14
  133.2 87.1 all-gather.16
  223.1 86.5 all-gather.18
  334.6 61.2 reduce-scatter.37
  399.8 97.9 reduce-scatter.35
  501.9 120.2 reduce-scatter.25
  626.3 120.2 reduce-scatter.21
  748.9 34.3 reduce-scatter.33
  786.0 15.3 reduce-scatter.29
  804.2 28.2 reduce-scatter.27
  834.6 28.3 reduce-scatter.31
  865.8 23.4 reduce-scatter.23
  893.3 86.9 all-reduce.5
  982.2 35.7 all-gather.22
  1019.9 24.8 all-gather.20
  1046.8 34.3 all-gather.24
where the time goes:
time: 1110 us; the launch traced here: 1100 us
  waiting for transfers between devices  804 us (72%)
  blocking collectives  104 us (9%)
  matrix products  73.8 us (7%)
  other arithmetic  45.3 us (4%)
  local copies, waits for them, and re-layouts  43.6 us (4%)
  between operations  20.3 us (2%)
    unnamed x24, waiting for transfers between devices  238 us
    reduce_scatter x1, waiting for transfers between devices, shards(): lax.psum_scatter(grads[3].astype(jnp.bfloat16), 'shard', scatter_dimensio...  122 us
    reduce_scatter x1, waiting for transfers between devices, shards(): lax.psum_scatter(grads[2].astype(jnp.bfloat16), 'shard', scatter_dimensio...  122 us
    all_gather x1, waiting for transfers between devices, shards(): lax.all_gather(w_fc1.astype(jnp.bfloat16), 'shard', axis=0, tiled=True)  86.1 us
    all_gather x1, waiting for transfers between devices, shards(): lax.all_gather(w_fc2.astype(jnp.bfloat16), 'shard', axis=0, tiled=True)  83.5 us
    dot_general x17, matrix products, product(): return jnp.einsum(form, left, right, preferred_element_type=jnp.float32)  70.1 us
    psum x1, blocking collectives, shards(): lax.psum((bias_partial, weight_squares), ('rep', 'shard'))  40 us
    all_gather x1, waiting for transfers between devices, shards(): lax.all_gather(w_proj.astype(jnp.bfloat16), 'shard', axis=0, tiled=True)  38.2 us
  transfers between devices with their start and end apart: 18, of which 17 were waited for; matrix products, arithmetic and copies ran while one was open for 11% of the time, Pallas kernels for 0%

commit v1 on v0

--- a/solution.py
+++ b/solution.py
@@ -180,7 +180,23 @@
     cvec = cond + time_embed(timesteps, width)
     silu_c = jax.nn.silu(cvec).astype(jnp.bfloat16)
     ada_local = w_ada.astype(jnp.bfloat16)
-    silu_group = lax.all_gather(silu_c, "shard", axis=0, tiled=True)
+    size, here, extent = (lax.axis_size("shard"), lax.axis_index("shard"), silu_c.shape[0])
+    upward = [(i_2, (i_2 + 1) % size) for i_2 in range(size)]
+    backward = [(i_2, (i_2 - 1) % size) for i_2 in range(size)]
+    silu_group = jnp.zeros((*silu_c.shape[:0], size * extent, *silu_c.shape[0 + 1 :]), silu_c.dtype)
+    silu_group = lax.dynamic_update_slice_in_dim(silu_group, silu_c, here * extent, axis=0)
+    from_left = from_right = silu_c
+    middle = size // 2
+    for step in range(1, middle + 1):
+        from_left = lax.ppermute(from_left, "shard", upward)
+        silu_group = lax.dynamic_update_slice_in_dim(
+            silu_group, from_left, (here - step) % size * extent, axis=0
+        )
+        if step < size - middle:
+            from_right = lax.ppermute(from_right, "shard", backward)
+            silu_group = lax.dynamic_update_slice_in_dim(
+                silu_group, from_right, (here + step) % size * extent, axis=0
+            )
     mod_cols = jnp.dot(silu_group, ada_local, preferred_element_type=jnp.float32)
     mod = lax.all_to_all(mod_cols, "shard", split_axis=0, concat_axis=1, tiled=True) + b_ada
     wq_b, wp_b = (

time: 1110 us -> 1100 us (level)
  starting transfers between devices: 4.38 us -> 37.8 us
  blocking collectives: 104 us -> 79.6 us
    ppermute x0 -> x15, starting transfers between devices: none -> 32.9 us  [the longest x7 32.4 us: shards(): from_right = lax.ppermute(from_right, 'shard', backward)]
    all_gather x1 -> x0, blocking collectives: 24.2 us -> none  [shards(): silu_group = lax.all_gather(silu_c, 'shard', axis=0, tiled=True)]
    all_gather x1, waiting for transfers between devices: 31.5 us -> 9.55 us  [shards(): lax.all_gather(w_qkv.astype(jnp.bfloat16), 'shard', axis=0, tiled=True)]
    ppermute x0 -> x15, waiting for transfers between devices: none -> 13.2 us  [the longest x8 11.6 us: shards(): from_left = lax.ppermute(from_left, 'shard', upward)]
  transfers between devices with their start and end apart: 18 -> 33, of which waited for: 17 -> 30; matrix products, arithmetic and copies ran while one was open for 11% -> 11% of each run, Pallas kernels for 0% -> 0%
where the time goes in v1:
time: 1100 us
  waiting for transfers between devices  793 us (72%)
  blocking collectives  79.6 us (7%)
  matrix products  75.8 us (7%)
  local copies, waits for them, and re-layouts  44.5 us (4%)
  other arithmetic  44 us (4%)
  starting transfers between devices  37.8 us (3%)
  between operations  20.6 us (2%)
    unnamed x24, waiting for transfers between devices  238 us
    reduce_scatter x1, waiting for transfers between devices, shards(): lax.psum_scatter(grads[3].astype(jnp.bfloat16), 'shard', scatter_dimensio...  122 us
    reduce_scatter x1, waiting for transfers between devices, shards(): lax.psum_scatter(grads[2].astype(jnp.bfloat16), 'shard', scatter_dimensio...  122 us
    all_gather x1, waiting for transfers between devices, shards(): lax.all_gather(w_fc1.astype(jnp.bfloat16), 'shard', axis=0, tiled=True)  86.1 us
    all_gather x1, waiting for transfers between devices, shards(): lax.all_gather(w_fc2.astype(jnp.bfloat16), 'shard', axis=0, tiled=True)  83.5 us
    dot_general x17, matrix products, product(): return jnp.einsum(form, left, right, preferred_element_type=jnp.float32)  71.2 us
    psum x1, blocking collectives, shards(): lax.psum((bias_partial, weight_squares), ('rep', 'shard'))  40 us
    all_gather x1, waiting for transfers between devices, shards(): lax.all_gather(new_pieces[4], 'rep', axis=0, tiled=True)  36.4 us
  transfers between devices with their start and end apart: 33, of which 30 were waited for; matrix products, arithmetic and copies ran while one was open for 11% of the time, Pallas kernels for 0%

profile of v1, /device:TPU:0, one launch (start us, length us, event | category | flops | bytes accessed | tf_op | source)
XLA Modules:
  0.0 1095.6 jit_solution(556863045233779974)
XLA Ops:
  76.8 9.5 all-gather.12.cloned.1.call-done
  95.0 35.6 %all-gather.14.cloned.1.call-done = bf16[1152,1152]{1,0:T(8,128)(2,1)} async-done(((bf16[72,1152]{1,0:T(8,128)(2,1)}), bf16[1152,1152]{1,0:T(8,128)(2,1)}) %all-gather.14.cloned.1.call-update) | async-done | bytes 2654224 | tf_op jit(solution)/shard_map/all_gather | solution.py:204
  134.6 86.1 %all-gather.16.cloned.1.call-done = bf16[1152,4608]{1,0:T(8,128)(2,1)} async-done(((bf16[72,4608]{1,0:T(8,128)(2,1)}), bf16[1152,4608]{1,0:T(8,128)(2,1)}) %all-gather.16.cloned.1.call-update) | async-done | bytes 10616848 | tf_op jit(solution)/shard_map/all_gather | solution.py:207
  226.5 83.5 %all-gather.18.cloned.1.call-done = bf16[4608,1152]{1,0:T(8,128)(2,1)} async-done(((bf16[288,1152]{1,0:T(8,128)(2,1)}), bf16[4608,1152]{1,0:T(8,128)(2,1)}) %all-gather.18.cloned.1.call-update) | async-done | bytes 10616848 | tf_op jit(solution)/shard_map/all_gather | solution.py:208
  310.0 8.6 fusion.89
  323.4 7.9 fusion.19
  354.4 6.7 convolution_convert_fusion
  362.3 5.9 convolution_convert_fusion.1
  369.2 6.5 fusion.28
  378.9 9.4 all_to_all.29
  397.7 100.0 %reduce-scatter.36.cloned.1.call-done = bf16[72,3456]{1,0:T(8,128)(2,1)} async-done(((bf16[1152,3456]{1,0:T(8,128)(2,1)}), bf16[72,3456]{1,0:T(8,128)(2,1)}) %reduce-scatter.36.cloned.1.call-update) | async-done | bytes 497680
  500.4 121.7 %reduce-scatter.26.cloned.1.call-done = bf16[288,1152]{1,0:T(8,128)(2,1)} async-done(((bf16[4608,1152]{1,0:T(8,128)(2,1)}), bf16[288,1152]{1,0:T(8,128)(2,1)}) %reduce-scatter.26.cloned.1.call-update) | async-done | bytes 663568 | tf_op jit(solution)/shard_map/reduce_scatter | solution.py:232
  624.8 121.7 %reduce-scatter.22.cloned.1.call-done = bf16[72,4608]{1,0:T(8,128)(2,1)} async-done(((bf16[1152,4608]{1,0:T(8,128)(2,1)}), bf16[72,4608]{1,0:T(8,128)(2,1)}) %reduce-scatter.22.cloned.1.call-update) | async-done | bytes 663568 | tf_op jit(solution)/shard_map/reduce_scatter | solution.py:229
  750.2 33.1 %reduce-scatter.34.cloned.1.call-done = f32[576,432]{1,0:T(8,128)} async-done(((f32[1152,432]{1,0:T(8,128)}), f32[576,432]{1,0:T(8,128)}) %reduce-scatter.34.cloned.1.call-update) | async-done | bytes 995344
  785.8 15.5 %reduce-scatter.30.cloned.1.call-done = f32[576,72]{1,0:T(8,128)} async-done(((f32[1152,72]{1,0:T(8,128)}), f32[576,72]{1,0:T(8,128)}) %reduce-scatter.30.cloned.1.call-update) | async-done | bytes 165904
  804.7 27.8 %reduce-scatter.28.cloned.1.call-done = f32[1728,72]{1,0:T(8,128)} async-done(((f32[3456,72]{1,0:T(8,128)}), f32[1728,72]{1,0:T(8,128)}) %reduce-scatter.28.cloned.1.call-update) | async-done | bytes 497680
  837.8 25.2 %reduce-scatter.32.cloned.1.call-done = f32[576,288]{1,0:T(8,128)} async-done(((f32[1152,288]{1,0:T(8,128)}), f32[576,288]{1,0:T(8,128)}) %reduce-scatter.32.cloned.1.call-update) | async-done | bytes 663568
  867.2 22.1 %reduce-scatter.24.cloned.1.call-done = f32[72,2304]{1,0:T(8,128)} async-done(((f32[72,4608]{1,0:T(8,128)}), f32[72,2304]{1,0:T(8,128)}) %reduce-scatter.24.cloned.1.call-update) | async-done | bytes 663568 | tf_op jit(solution)/shard_map/reduce_scatter | solution.py:239
  893.2 40.0 %all-reduce.3 = (f32[]{:T(128)}, f32[16128]{0:T(1024)S(1)}) all-reduce(f32[]{:T(128)S(6)} %add.510, f32[16128]{0:T(1024)S(1)} %constant_dynamic-update-slice_fusion.10), channel_id=1, replica_groups=mesh['rep'=2,'shard'=16] {'rep','shard'}, use_global_device_ids=true, to_apply=%region_32.33 | all-reduce | flops 16129 | bytes 129032 | tf_op jit(solution)/shard_map/psum | solution.py:245
  949.4 30.7 %all-reduce.6.cloned.1.call-done = f32[16,1152]{1,0:T(8,128)} async-done(((f32[16,1152]{1,0:T(8,128)}), f32[16,1152]{1,0:T(8,128)}) %all-reduce.6.cloned.1.call-update) | async-done | bytes 73744
  985.1 21.1 %all-gather = f32[2,1728,72]{1,2,0:T(8,128)S(1)} all-gather(f32[1,1728,72]{1,2,0:T(8,128)S(1)} %get-tuple-element.56), channel_id=1, replica_groups=mesh['rep'=2,'shard'=16] {'rep'}, dimensions={0}, use_global_device_ids=true | all-gather | bytes 1492992 | tf_op jit(solution)/shard_map/all_gather | solution.py:265
  1009.5 9.2 all-gather.1
  1025.1 19.7 %all-gather.20.cloned.1.call-done = f32[72,4608]{1,0:T(8,128)} async-done(((f32[72,2304]{1,0:T(8,128)}), f32[72,4608]{1,0:T(8,128)}) %all-gather.20.cloned.1.call-update) | async-done | bytes 1327120 | tf_op jit(solution)/shard_map/all_gather | solution.py:267
  1044.7 36.4 %all-gather.24.cloned.1.call-done = f32[2,576,432]{1,2,0:T(8,128)} async-done(((f32[1,576,432]{1,2,0:T(8,128)}), f32[2,576,432]{1,2,0:T(8,128)}) %all-gather.24.cloned.1.call-update) | async-done | bytes 1990672 | tf_op jit(solution)/shard_map/all_gather | solution.py:269
  (326 shorter events, 191.1 us)
Async XLA Ops:
  7.2 79.1 %all-gather.12.cloned.1.call-start = ((), (), s32[]{:S(2)}) async-start(), calls=%async_computation.11 | async-start | bytes 8460288 | tf_op jit(solution)/shard_map/all_gather | solution.py:203
  9.4 121.2 %all-gather.14.cloned.1.call-start = ((), (), s32[]{:S(2)}) async-start(), calls=%async_computation.12 | async-start | bytes 2820096 | tf_op jit(solution)/shard_map/all_gather | solution.py:204
  11.2 209.5 %all-gather.16.cloned.1.call-start = ((), (), s32[]{:S(2)}) async-start(), calls=%async_computation.13 | async-start | bytes 11280384 | tf_op jit(solution)/shard_map/all_gather | solution.py:207
  12.2 297.8 %all-gather.18.cloned.1.call-start = ((), (), s32[]{:S(2)}) async-start(), calls=%async_computation.14 | async-start | bytes 11280384 | tf_op jit(solution)/shard_map/all_gather | solution.py:208
  16.1 6.7 collective-permute-start
  16.6 6.5 collective-permute-start.1
  28.9 6.1 collective-permute-start.5
  34.9 6.0 collective-permute-start.7
  52.5 7.0 collective-permute-start.13
  58.3 6.1 collective-permute-start.14
  65.5 10.5 all-to-all-start
  69.0 326.8 %reduce-scatter.38.cloned.1.call-start = ((), (), s32[]{:S(2)}) async-start(), calls=%async_computation.27 | async-start | bytes 2820096
  334.4 163.3 %reduce-scatter.36.cloned.1.call-start = ((), (), s32[]{:S(2)}) async-start(), calls=%async_computation.26 | async-start | bytes 8460288
  354.3 267.8 %reduce-scatter.26.cloned.1.call-start = ((), (), s32[]{:S(2)}) async-start(), calls=%async_computation.17 | async-start | bytes 11280384 | tf_op jit(solution)/shard_map/reduce_scatter | solution.py:232
  361.1 385.5 %reduce-scatter.22.cloned.1.call-start = ((), (), s32[]{:S(2)}) async-start(), calls=%async_computation.15 | async-start | bytes 11280384 | tf_op jit(solution)/shard_map/reduce_scatter | solution.py:229
  368.3 415.0 %reduce-scatter.34.cloned.1.call-start = ((), (), s32[]{:S(2)}) async-start(), calls=%async_computation.24 | async-start | bytes 3538944
  390.3 411.0 %reduce-scatter.30.cloned.1.call-start = ((), (), s32[]{:S(2)}) async-start(), calls=%async_computation.22 | async-start | bytes 884736
  397.7 434.8 %reduce-scatter.28.cloned.1.call-start = ((), (), s32[]{:S(2)}) async-start(), calls=%async_computation.21 | async-start | bytes 2654208
  500.3 362.6 %reduce-scatter.32.cloned.1.call-start = ((), (), s32[]{:S(2)}) async-start(), calls=%async_computation.23 | async-start | bytes 2654208
  624.8 264.5 %reduce-scatter.24.cloned.1.call-start = ((), (), s32[]{:S(2)}) async-start(), calls=%async_computation.16 | async-start | bytes 1990656 | tf_op jit(solution)/shard_map/reduce_scatter | solution.py:239
  748.8 231.3 %all-reduce.6.cloned.1.call-start = ((), (), s32[]{:S(2)}) async-start(), calls=%async_computation.25 | async-start | bytes 147456
  893.1 127.4 %all-gather.22.cloned.1.call-start = ((), (), s32[]{:S(2)}) async-start(), calls=%async_computation.19 | async-start | bytes 2211840 | tf_op jit(solution)/shard_map/all_gather | solution.py:268
  939.0 105.7 %all-gather.20.cloned.1.call-start = ((), (), s32[]{:S(2)}) async-start(), calls=%async_computation.18 | async-start | bytes 1990656 | tf_op jit(solution)/shard_map/all_gather | solution.py:267
  943.0 138.1 %all-gather.24.cloned.1.call-start = ((), (), s32[]{:S(2)}) async-start(), calls=%async_computation.20 | async-start | bytes 3317760 | tf_op jit(solution)/shard_map/all_gather | solution.py:269
  (77 other events, 1478.8 us)
Sparse Core Ops, SparseCore 0:
  10.8 75.5 all-gather.11
  89.1 41.4 all-gather.13
  133.5 87.1 all-gather.15
  223.4 86.5 all-gather.17
  334.6 61.1 reduce-scatter.37
  399.7 98.0 reduce-scatter.35
  501.8 120.2 reduce-scatter.25
  626.2 120.3 reduce-scatter.21
  748.8 34.3 reduce-scatter.33
  785.9 15.3 reduce-scatter.29
  804.2 28.2 reduce-scatter.27
  834.6 28.3 reduce-scatter.31
  865.8 23.4 reduce-scatter.23
  893.3 86.8 all-reduce.5
  982.1 35.6 all-gather.21
  1019.8 24.8 all-gather.19
  1046.7 34.3 all-gather.23
